TPU v7x, 512 devices: a whole 4x8x8 slice. The times are simulated.
512 devices in a mesh: gx: 8 (over z_hi, core), gy: 8 (over y), gz: 8 (over x, z_lo).
Axes of the slice: x: 4, y: 8, z: 8 (z_hi: 4, z_lo: 2; z = z_hi * 2 + z_lo), core: 2. Of those that a mesh axis runs over, the one named last changes fastest.
Arguments:
- features: bfloat16 [8, 8, 8, 128, 128], P('gx', 'gy', 'gz'), may hold values from -6 to 6
- positions: float32 [8, 8, 8, 3, 128], P('gx', 'gy', 'gz'), may hold values from 0 to 1
- counts: int32 [8, 8, 8], P('gx', 'gy', 'gz'), may hold values from 1 to 128, as said below
- w_proj: bfloat16 [4, 128, 128], replicated, may hold values from -0.5 to 0.5
- w_mix: bfloat16 [128, 128], replicated, may hold values from -0.5 to 0.5
- w_long: bfloat16 [64, 128], replicated, may hold values from -0.75 to 0.75
- w_charge: bfloat16 [64, 128], replicated, may hold values from -0.5 to 0.5
- charge_bias: float32 [64], replicated, may hold values from -4 to 4
- w_energy: float32 [128], replicated, may hold values from -0.5 to 0.5
- k_filter: float32 [64, 2048], replicated, may hold values from 0.1 to 1
- k_index: int32 [3, 2048], replicated, may hold values from -6 to 6
Outputs:
- updated: bfloat16 [8, 8, 8, 128, 128], P('gx', 'gy', 'gz')
- energies: float32 [8, 8, 8, 128], P('gx', 'gy', 'gz')
- forces: float32 [8, 8, 8, 3, 128], P('gx', 'gy', 'gz')
Inputs may be any that keep to these rules, and one draw needn't show every extreme that they name: Slots 0 to counts[x,y,z] - 1 of cell (x,y,z) hold live atoms, the rest are padding; some cell holds 128 live atoms.
All inputs are finite; a program needn't handle non-finite values.
Results may differ from a plain program's by a relative error of at most 0.0068.
Values may be sent and summed in bfloat16 or wider, within the bound.
A program may use at most 64 MiB of HBM per device.

v0:
```python
import math
import jax
import jax.numpy as jnp
from jax import lax
from jax.sharding import PartitionSpec as P

CUTOFF = 0.9
GAMMAS = (1.0, 3.0, 8.0, 20.0)
PRECISE = lax.Precision.HIGHEST
CONTRACT_LAST = (((1,), (1,)), ((), ()))
CONTRACT_FIRST = (((0,), (0,)), ((), ()))


def extended(value, sides, width):
    for axis, dim in sides:
        peers, length = (lax.axis_size(axis), value.shape[dim])
        up = [(i, (i + 1) % peers) for i in range(peers)]
        down = [(j, i) for i, j in up]
        last = lax.slice_in_dim(value, length - width, length, axis=dim)
        initial = lax.slice_in_dim(value, 0, width, axis=dim)
        before = lax.ppermute(last, axis, up)
        after = lax.ppermute(initial, axis, down)
        value = jnp.concatenate([before, value, after], axis=dim)
    return value


def silu_grad(values):
    sigma = jax.nn.sigmoid(values)
    return sigma * (1.0 + values * (1.0 - sigma))


def pair_geometry(centre, others, neighbour):
    cell_shift = (
        jnp.stack([neighbour // 9, neighbour // 3 % 3, neighbour % 3]).astype(jnp.float32) - 1.0
    )
    offset_vec = others[:, None, :] + cell_shift[:, None, None] - centre[:, :, None]
    scaled = jnp.sum(offset_vec * offset_vec, axis=0) / (CUTOFF * CUTOFF)
    atom_count = centre.shape[1]
    slot_ids = jnp.arange(atom_count, dtype=jnp.int32)
    self_pair = (slot_ids[:, None] == slot_ids[None, :]) & (neighbour == 13)
    keep_mask = jnp.where(self_pair, 0.0, 1.0).astype(jnp.float32)
    envelope_base = jnp.maximum(1.0 - scaled, 0.0)
    decay_rates = jnp.asarray(GAMMAS, dtype=jnp.float32)[None, :, None]
    decay_terms = jnp.exp(-decay_rates * scaled[:, None, :]) * keep_mask[:, None, :]
    envelope = (envelope_base * envelope_base)[:, None, :]
    radial = decay_terms * envelope
    radial_slope = decay_terms * (-decay_rates * envelope - 2.0 * envelope_base[:, None, :])
    return (offset_vec, radial, radial_slope)


def phases(absolute, wave_vec, first_wave, wave_block):
    wave_part = wave_vec[:, first_wave : first_wave + wave_block]
    phase_angle = (
        absolute[0][:, None] * wave_part[0][None, :]
        + absolute[1][:, None] * wave_part[1][None, :]
        + absolute[2][:, None] * wave_part[2][None, :]
    )
    return (jnp.cos(phase_angle), jnp.sin(phase_angle))


def structure(weights_rows, absolute, wave_vec, wave_block):
    cosine_parts = []
    sine_parts = []
    for first_wave in range(0, wave_vec.shape[1], wave_block):
        cosine, sine_part = phases(absolute, wave_vec, first_wave, wave_block)
        cosine_parts.append(jnp.dot(weights_rows, cosine, precision=PRECISE))
        sine_parts.append(jnp.dot(weights_rows, sine_part, precision=PRECISE))
    return (jnp.concatenate(cosine_parts, axis=1), jnp.concatenate(sine_parts, axis=1))


def shards(
    features,
    positions,
    counts,
    w_proj,
    w_mix,
    w_long,
    w_charge,
    charge_bias,
    w_energy,
    k_filter,
    k_index,
):
    own_rows = features[0, 0, 0]
    centre = positions[0, 0, 0]
    atom_count, channels = own_rows.shape
    basis_count = w_proj.shape[0]
    waves = k_index.shape[1]
    wave_block = min(512, waves)
    grid_sizes = (lax.axis_size("gx"), lax.axis_size("gy"), lax.axis_size("gz"))
    scale_long = 4.0 / math.sqrt(atom_count * grid_sizes[0] * grid_sizes[1] * grid_sizes[2] * waves)
    cell_anchor = jnp.stack(
        [lax.axis_index("gx"), lax.axis_index("gy"), lax.axis_index("gz")]
    ).astype(jnp.float32)
    living = (jnp.arange(atom_count, dtype=jnp.int32) < counts[0, 0, 0]).astype(jnp.float32)
    masked = own_rows * living[:, None].astype(jnp.bfloat16)
    extent = jnp.asarray(grid_sizes, dtype=jnp.float32)
    wave_vec = 2.0 * math.pi * k_index.astype(jnp.float32) / extent[:, None]
    absolute = centre + cell_anchor[:, None]
    charges = (
        jax.nn.silu(
            lax.dot_general(w_charge, masked, CONTRACT_LAST, preferred_element_type=jnp.float32)
            + charge_bias[:, None]
        )
        * living[None, :]
    )
    stacked_rows = jnp.concatenate([charges, living[None, :]], axis=0)
    local_c, local_s = structure(stacked_rows, absolute, wave_vec, wave_block)
    totals = lax.psum(
        (local_c, local_s, jnp.sum(charges, axis=1), jnp.sum(living)), ("gx", "gy", "gz")
    )
    charge_mean = totals[2] / totals[3]
    neutral = (charges - charge_mean[:, None]) * living[None, :]
    row_count = charges.shape[0]
    struct_c = totals[0][:row_count] - charge_mean[:, None] * totals[0][row_count:]
    struct_s = totals[1][:row_count] - charge_mean[:, None] * totals[1][row_count:]
    near_pos = extended(positions, (("gx", 0), ("gy", 1), ("gz", 2)), 1).reshape(27, 3, atom_count)
    local_proj = jnp.einsum(
        "jc,bcd->bjd", masked, w_proj, preferred_element_type=jnp.float32
    ).astype(jnp.bfloat16)
    near_feat = extended(masked[None, None, None], (("gx", 0), ("gy", 1), ("gz", 2)), 1).reshape(
        27, atom_count, channels
    )

    def fetch_basis(neighbour):
        near_rows = lax.dynamic_index_in_dim(near_feat, neighbour, 0, keepdims=False)
        return (
            jnp.einsum("jc,bcd->bjd", near_rows, w_proj, preferred_element_type=jnp.float32)
            .astype(jnp.bfloat16)
            .reshape(basis_count * atom_count, channels)
        )

    def add_message(neighbour, message):
        others = lax.dynamic_index_in_dim(near_pos, neighbour, 0, keepdims=False)
        offset_vec, radial, radial_slope = pair_geometry(centre, others, neighbour)
        return message + jnp.dot(
            radial.astype(jnp.bfloat16).reshape(atom_count, -1),
            fetch_basis(neighbour),
            preferred_element_type=jnp.float32,
        )

    message = lax.fori_loop(0, 27, add_message, jnp.zeros((atom_count, channels), jnp.float32))
    filtered_cos = k_filter * struct_c
    filtered_sin = k_filter * struct_s
    potential = jnp.zeros(charges.shape, jnp.float32)
    for first_wave in range(0, waves, wave_block):
        cosine, sine_part = phases(absolute, wave_vec, first_wave, wave_block)
        potential = (
            potential
            + lax.dot_general(
                filtered_cos[:, first_wave : first_wave + wave_block],
                cosine,
                CONTRACT_LAST,
                precision=PRECISE,
            )
            + lax.dot_general(
                filtered_sin[:, first_wave : first_wave + wave_block],
                sine_part,
                CONTRACT_LAST,
                precision=PRECISE,
            )
        )
    potential = scale_long * potential
    pre_act = jnp.dot(
        message.astype(jnp.bfloat16), w_mix, preferred_element_type=jnp.float32
    ) + lax.dot_general(
        potential.astype(jnp.bfloat16), w_long, CONTRACT_FIRST, preferred_element_type=jnp.float32
    )
    refined = own_rows.astype(jnp.float32) + jax.nn.silu(pre_act)
    energy = living * jnp.sum(jax.nn.silu(refined) * w_energy[None, :], axis=1)
    grad_new = living[:, None] * w_energy[None, :] * silu_grad(refined)
    grad_pre = (grad_new * silu_grad(pre_act)).astype(jnp.bfloat16)
    adjoint = lax.dot_general(
        grad_pre, w_mix, CONTRACT_LAST, preferred_element_type=jnp.float32
    ).astype(jnp.bfloat16)
    pull_back = lax.dot_general(w_long, grad_pre, CONTRACT_LAST, preferred_element_type=jnp.float32)
    near_adjoint = extended(
        adjoint[None, None, None], (("gx", 0), ("gy", 1), ("gz", 2)), 1
    ).reshape(27, atom_count, channels)
    pull_c, pull_s = structure(pull_back, absolute, wave_vec, wave_block)
    back_c, back_s = lax.psum((pull_c, pull_s), ("gx", "gy", "gz"))

    def add_force(neighbour, near_force):
        others = lax.dynamic_index_in_dim(near_pos, neighbour, 0, keepdims=False)
        offset_vec, radial, radial_slope = pair_geometry(centre, others, neighbour)
        first_term = lax.dot_general(
            adjoint, fetch_basis(neighbour), CONTRACT_LAST, preferred_element_type=jnp.float32
        ).reshape(atom_count, basis_count, atom_count)
        near_rows = lax.dynamic_index_in_dim(near_adjoint, neighbour, 0, keepdims=False)
        second_term = jnp.einsum(
            "bic,jc->ibj", local_proj, near_rows, preferred_element_type=jnp.float32
        )
        strength = jnp.sum(radial_slope * (first_term + second_term), axis=1)
        return near_force + 2.0 / (CUTOFF * CUTOFF) * jnp.sum(
            strength[None, :, :] * offset_vec, axis=2
        )

    near_force = lax.fori_loop(0, 27, add_force, jnp.zeros((3, atom_count), jnp.float32))
    mixing = jnp.concatenate([pull_back, neutral], axis=0)
    weights_along = jnp.concatenate([filtered_sin, k_filter * back_s], axis=0)
    weights_across = jnp.concatenate([filtered_cos, k_filter * back_c], axis=0)
    ewald_grad = jnp.zeros((3, atom_count), jnp.float32)
    for first_wave in range(0, waves, wave_block):
        cosine, sine_part = phases(absolute, wave_vec, first_wave, wave_block)
        along_term = lax.dot_general(
            mixing,
            weights_along[:, first_wave : first_wave + wave_block],
            CONTRACT_FIRST,
            precision=PRECISE,
        )
        across_term = lax.dot_general(
            mixing,
            weights_across[:, first_wave : first_wave + wave_block],
            CONTRACT_FIRST,
            precision=PRECISE,
        )
        ewald_grad = ewald_grad + lax.dot_general(
            wave_vec[:, first_wave : first_wave + wave_block],
            cosine * along_term - sine_part * across_term,
            CONTRACT_LAST,
            precision=PRECISE,
        )
    forces = near_force - scale_long * ewald_grad
    return (
        refined.astype(jnp.bfloat16)[None, None, None],
        energy[None, None, None],
        forces[None, None, None],
    )


def solution(mesh):
    in_specs = (
        P("gx", "gy", "gz", None, None),
        P("gx", "gy", "gz", None, None),
        P("gx", "gy", "gz"),
        P(),
        P(),
        P(),
        P(),
        P(),
        P(),
        P(),
        P(),
    )
    out_specs = (
        P("gx", "gy", "gz", None, None),
        P("gx", "gy", "gz", None),
        P("gx", "gy", "gz", None, None),
    )
    return jax.shard_map(shards, mesh=mesh, in_specs=in_specs, out_specs=out_specs, check_vma=False)
```

profile of v0, /device:TPU:23, one launch (start us, length us, event | category | flops | bytes accessed | tf_op | source)
XLA Modules:
  0.0 663.8 jit_solution(11404104133226041706)
XLA Ops:
  7.2 6.4 collective-permute-start
  13.6 1.9 collective-permute-start.1
  17.1 6.6 collective-permute-start.7
  23.7 1.9 collective-permute-start.6
  39.9 98.9 %all-reduce = (f32[64]{0:T(128)S(1)}, f32[]{:T(128)}) all-reduce(f32[64]{0:T(128)S(1)} %get-tuple-element.752, f32[]{:T(128)} %fusion.291), channel_id=1, replica_groups=mesh['gx'=8,'gy'=8,'gz'=8] {'gx','gy','gz'}, use_global_device_ids=true, to_apply=%region_5.6 | all-reduce | flops 65 | bytes 520 | tf_op jit(solution)/shard_map/psum | solution.py:109
  139.5 2.1 collective-permute-start.3
  141.6 3.5 collective-permute-start.2
  145.2 1.9 collective-permute-start.9
  147.1 4.6 collective-permute-start.8
  151.7 1.9 collective-permute-start.5
  153.7 3.4 collective-permute-start.4
  157.1 2.8 collective-permute-start.11
  159.9 3.5 collective-permute-start.10
  163.6 2.9 collective-permute-done.11
  166.6 6.0 collective-permute-done.10
  173.3 20.3 %while.36 = (s32[]{:T(128)}, f32[128,128]{1,0:T(8,128)S(1)}, f32[27,3,128]{2,1,0:T(4,128)S(1)}, f32[1,1,1,3,128]{4,3,2,1,0:T(4,128)S(1)}, bf16[27,128,128]{2,1,0...) while((s32[]{:T(128)}, f32[128,128]{1,0:T(8,128)S(1)}, ...), condition=%wide.region_2.3_spmd.clone.clone, body=%wide.region_0.0_spmd.clone.clone.sunk | while | flops 34161064 | bytes 826287 | solution.py:142
  193.8 123.2 %all-reduce.8.cloned.1.call-done = (f32[65,2048]{1,0:T(8,128)}, f32[65,2048]{1,0:T(8,128)}) async-done(((f32[65,2048]{1,0:T(8,128)}, f32[65,2048]{1,0:T(8,128)}), (f32[65,2048]{1,0:T(8,128)}, f32[65,2048]{1,0:T(8,128)})) %all-reduce.8.cloned.1.call-update) | async-done | bytes 1064976 | tf_op jit(solution)/shard_map/psum | solution.py:109
  318.7 1.4 fusion.48
  322.7 1.3 convolution_add_fusion.7
  325.4 1.3 convolution_add_fusion.5
  328.0 1.3 convolution_add_fusion.3
  331.6 1.9 collective-permute-start.13
  333.5 4.7 collective-permute-start.12
  348.0 1.9 collective-permute-start.15
  349.9 3.4 collective-permute-start.14
  356.1 3.4 collective-permute-start.17
  359.5 2.1 collective-permute-start.16
  364.4 2.7 collective-permute-done.17
  367.0 6.8 %collective-permute-done.16 = bf16[3,3,1,128,128]{4,3,2,1,0:T(8,128)(2,1)} collective-permute-done((bf16[3,3,1,128,128]{4,3,2,1,0:T(8,128)(2,1)}, bf16[3,3,1,128,128]{4,3,2,1,0:T(8,128)(2,1)}, u32[]{:S(2)}, u32[]{:S(2)}) %collective-permute-start.16) | collective-permute-done | bytes 294944 | tf_op jit(solution)/shard_map/ppermute | solution.py:21
  373.8 2.0 pad_maximum_fusion.1
  375.8 67.3 %while.37 = (s32[]{:T(128)}, f32[3,128]{1,0:T(4,128)S(1)}, f32[27,3,128]{2,1,0:T(4,128)S(1)}, f32[1,1,1,3,128]{4,3,2,1,0:T(4,128)S(1)}, bf16[27,128,128]{2,1,0:T...) while((s32[]{:T(128)}, f32[3,128]{1,0:T(4,128)S(1)}, ...), condition=%wide.region_14.15_spmd.clone.clone, body=%wide.region_10.14_spmd.clone.clone.sunk | while | flops 51315852 | bytes 2604507 | solution.py:198
  443.1 199.9 %all-reduce.6.cloned.1.call-done = (f32[64,2048]{1,0:T(8,128)}, f32[64,2048]{1,0:T(8,128)}) async-done(((f32[64,2048]{1,0:T(8,128)}, f32[64,2048]{1,0:T(8,128)}), (f32[64,2048]{1,0:T(8,128)}, f32[64,2048]{1,0:T(8,128)})) %all-reduce.6.cloned.1.call-update) | async-done | bytes 1048592 | tf_op jit(solution)/shard_map/psum | solution.py:181
  (715 shorter events, 134.4 us)
Async XLA Ops:
  7.2 309.8 %all-reduce.8.cloned.1.call-start = ((), (), s32[]{:S(2)}) async-start(), calls=%async_computation.1 | async-start | bytes 2359296 | tf_op jit(solution)/shard_map/psum | solution.py:109
  7.2 132.2 %collective-permute-start = (f32[1,1,1,3,128]{4,2,3,1,0:T(1,128)}, f32[1,1,1,3,128]{4,2,3,1,0:T(1,128)S(1)}, u32[]{:S(2)}, u32[]{:S(2)}) collective-permute-start(f32[1,1,1,3,128]{4,2,3,1,0:T(1,128)} %param.19), channel_id=1, source_target_pairs={{0,64},{64,128},{128,192},{192,256},{256,320},{320,384},{384,448},... | collective-permute-start | bytes 4616 | tf_op jit(solution)/shard_map/ppermute | solution.py:21
  13.6 125.9 %collective-permute-start.1 = (f32[1,1,1,3,128]{4,2,3,1,0:T(1,128)}, f32[1,1,1,3,128]{4,2,3,1,0:T(1,128)S(1)}, u32[]{:S(2)}, u32[]{:S(2)}) collective-permute-start(f32[1,1,1,3,128]{4,2,3,1,0:T(1,128)} %param.19), channel_id=1, source_target_pairs={{64,0},{128,64},{192,128},{256,192},{320,256},{384,320},{448,384},... | collective-permute-start | bytes 4616 | tf_op jit(solution)/shard_map/ppermute | solution.py:22
  17.1 128.0 %collective-permute-start.7 = (bf16[1,1,1,128,128]{4,3,2,1,0:T(8,128)(2,1)S(1)}, bf16[1,1,1,128,128]{4,3,2,1,0:T(8,128)(2,1)S(1)}, u32[]{:S(2)}, u32[]{:S(2)}) collective-permute-start(bf16[1,1,1,128,128]{4,3,2,1,0:T(8,128)(2,1)S(1)} %broadcast_multiply_fusion.2), channel_id=1, source_target_pairs={{64,0},{128,64},{192,128},{256,192},{320,256},{384,320},{448,384},... | collective-permute-start | bytes 98312 | tf_op jit(solution)/shard_map/ppermute | solution.py:22
  23.7 121.4 %collective-permute-start.6 = (bf16[1,1,1,128,128]{4,3,2,1,0:T(8,128)(2,1)S(1)}, bf16[1,1,1,128,128]{4,3,2,1,0:T(8,128)(2,1)S(1)}, u32[]{:S(2)}, u32[]{:S(2)}) collective-permute-start(bf16[1,1,1,128,128]{4,3,2,1,0:T(8,128)(2,1)S(1)} %broadcast_multiply_fusion.2), channel_id=1, source_target_pairs={{0,64},{64,128},{128,192},{192,256},{256,320},{320,384},{384,448},... | collective-permute-start | bytes 98312 | tf_op jit(solution)/shard_map/ppermute | solution.py:21
  25.9 316.2 %copy-start.26 = (f32[1,512]{1,0:T(1,128)}, f32[1,512]{1,0:T(1,128)S(1)}, u32[]{:S(2)}) copy-start(f32[1,512]{1,0:T(1,128)S(1)} %get-tuple-element.737) | copy-start | bytes 6148
  25.9 316.2 %copy-start.29 = (f32[1,512]{1,0:T(1,128)}, f32[1,512]{1,0:T(1,128)S(1)}, u32[]{:S(2)}) copy-start(f32[1,512]{1,0:T(1,128)S(1)} %get-tuple-element.747) | copy-start | bytes 6148
  25.9 317.5 %copy-start.8 = (f32[1,512]{1,0:T(1,128)}, f32[1,512]{1,0:T(1,128)S(1)}, u32[]{:S(2)}) copy-start(f32[1,512]{1,0:T(1,128)S(1)} %get-tuple-element.738) | copy-start | bytes 6148
  25.9 317.5 %copy-start.10 = (f32[1,512]{1,0:T(1,128)}, f32[1,512]{1,0:T(1,128)S(1)}, u32[]{:S(2)}) copy-start(f32[1,512]{1,0:T(1,128)S(1)} %get-tuple-element.739) | copy-start | bytes 6148
  25.9 317.5 %copy-start.12 = (f32[1,512]{1,0:T(1,128)}, f32[1,512]{1,0:T(1,128)S(1)}, u32[]{:S(2)}) copy-start(f32[1,512]{1,0:T(1,128)S(1)} %get-tuple-element.740) | copy-start | bytes 6148
  25.9 318.7 %copy-start.14 = (f32[1,512]{1,0:T(1,128)}, f32[1,512]{1,0:T(1,128)S(1)}, u32[]{:S(2)}) copy-start(f32[1,512]{1,0:T(1,128)S(1)} %get-tuple-element.741) | copy-start | bytes 6148
  25.9 318.7 %copy-start.16 = (f32[1,512]{1,0:T(1,128)}, f32[1,512]{1,0:T(1,128)S(1)}, u32[]{:S(2)}) copy-start(f32[1,512]{1,0:T(1,128)S(1)} %get-tuple-element.742) | copy-start | bytes 6148
  25.9 318.7 %copy-start.18 = (f32[1,512]{1,0:T(1,128)}, f32[1,512]{1,0:T(1,128)S(1)}, u32[]{:S(2)}) copy-start(f32[1,512]{1,0:T(1,128)S(1)} %get-tuple-element.743) | copy-start | bytes 6148
  25.9 320.7 %copy-start.20 = (f32[1,512]{1,0:T(1,128)}, f32[1,512]{1,0:T(1,128)S(1)}, u32[]{:S(2)}) copy-start(f32[1,512]{1,0:T(1,128)S(1)} %get-tuple-element.744) | copy-start | bytes 6148
  26.0 320.7 %copy-start.22 = (f32[1,512]{1,0:T(1,128)}, f32[1,512]{1,0:T(1,128)S(1)}, u32[]{:S(2)}) copy-start(f32[1,512]{1,0:T(1,128)S(1)} %get-tuple-element.745) | copy-start | bytes 6148
  26.0 320.7 %copy-start.24 = (f32[1,512]{1,0:T(1,128)}, f32[1,512]{1,0:T(1,128)S(1)}, u32[]{:S(2)}) copy-start(f32[1,512]{1,0:T(1,128)S(1)} %get-tuple-element.746) | copy-start | bytes 6148
  26.8 326.5 %copy-start.5 = (f32[128]{0:T(128)}, f32[128]{0:T(128)S(1)}, u32[]{:S(2)}) copy-start(f32[128]{0:T(128)S(1)} %get-tuple-element.751) | copy-start | bytes 1540
  38.8 604.2 %all-reduce.6.cloned.1.call-start = ((), (), s32[]{:S(2)}) async-start(), calls=%async_computation | async-start | bytes 2097152 | tf_op jit(solution)/shard_map/psum | solution.py:181
  139.5 12.2 %collective-permute-start.3 = (f32[3,1,1,3,128]{4,2,3,1,0:T(1,128)S(1)}, f32[3,1,1,3,128]{4,2,3,1,0:T(1,128)S(1)}, u32[]{:S(2)}, u32[]{:S(2)}) collective-permute-start(f32[3,1,1,3,128]{4,2,3,1,0:T(1,128)S(1)} %constant_dynamic-update-slice_fusion), channel_id=1, source_target_pairs={{8,0},{16,8},{24,16},{32,24},{40,32},{48,40},{56,48},{0,56},{9,1},... | collective-permute-start | bytes 13832 | tf_op jit(solution)/shard_map/ppermute | solution.py:22
  141.6 10.1 %collective-permute-start.2 = (f32[3,1,1,3,128]{4,2,3,1,0:T(1,128)S(1)}, f32[3,1,1,3,128]{4,2,3,1,0:T(1,128)S(1)}, u32[]{:S(2)}, u32[]{:S(2)}) collective-permute-start(f32[3,1,1,3,128]{4,2,3,1,0:T(1,128)S(1)} %constant_dynamic-update-slice_fusion), channel_id=1, source_target_pairs={{0,8},{8,16},{16,24},{24,32},{32,40},{40,48},{48,56},{56,0},{1,9},... | collective-permute-start | bytes 13832 | tf_op jit(solution)/shard_map/ppermute | solution.py:21
  145.2 11.9 %collective-permute-start.9 = (bf16[3,1,1,128,128]{4,3,2,1,0:T(8,128)(2,1)S(1)}, bf16[3,1,1,128,128]{4,3,2,1,0:T(8,128)(2,1)S(1)}, u32[]{:S(2)}, u32[]{:S(2)}) collective-permute-start(bf16[3,1,1,128,128]{4,3,2,1,0:T(8,128)(2,1)S(1)} %pad_maximum_fusion.12), channel_id=1, source_target_pairs={{8,0},{16,8},{24,16},{32,24},{40,32},{48,40},{56,48},{0,56},{9,1},... | collective-permute-start | bytes 294920 | tf_op jit(solution)/shard_map/ppermute | solution.py:22
  147.1 9.9 %collective-permute-start.8 = (bf16[3,1,1,128,128]{4,3,2,1,0:T(8,128)(2,1)S(1)}, bf16[3,1,1,128,128]{4,3,2,1,0:T(8,128)(2,1)S(1)}, u32[]{:S(2)}, u32[]{:S(2)}) collective-permute-start(bf16[3,1,1,128,128]{4,3,2,1,0:T(8,128)(2,1)S(1)} %pad_maximum_fusion.12), channel_id=1, source_target_pairs={{0,8},{8,16},{16,24},{24,32},{32,40},{40,48},{48,56},{56,0},{1,9},... | collective-permute-start | bytes 294920 | tf_op jit(solution)/shard_map/ppermute | solution.py:21
  151.7 11.8 %collective-permute-start.5 = (f32[3,3,1,3,128]{4,2,3,1,0:T(1,128)S(1)}, f32[3,3,1,3,128]{4,2,3,1,0:T(1,128)S(1)}, u32[]{:S(2)}, u32[]{:S(2)}) collective-permute-start(f32[3,3,1,3,128]{4,2,3,1,0:T(1,128)S(1)} %pad_maximum_fusion.17), channel_id=1, source_target_pairs={{1,0},{2,1},{3,2},{4,3},{5,4},{6,5},{7,6},{0,7},{9,8},{10,9},{11,1... | collective-permute-start | bytes 41480 | tf_op jit(solution)/shard_map/ppermute | solution.py:22
  153.7 9.9 %collective-permute-start.4 = (f32[3,3,1,3,128]{4,2,3,1,0:T(1,128)S(1)}, f32[3,3,1,3,128]{4,2,3,1,0:T(1,128)S(1)}, u32[]{:S(2)}, u32[]{:S(2)}) collective-permute-start(f32[3,3,1,3,128]{4,2,3,1,0:T(1,128)S(1)} %pad_maximum_fusion.17), channel_id=1, source_target_pairs={{0,1},{1,2},{2,3},{3,4},{4,5},{5,6},{6,7},{7,0},{8,9},{9,10},{10,1... | collective-permute-start | bytes 41480 | tf_op jit(solution)/shard_map/ppermute | solution.py:21
  157.1 9.5 %collective-permute-start.11 = (bf16[3,3,1,128,128]{4,3,2,1,0:T(8,128)(2,1)S(1)}, bf16[3,3,1,128,128]{4,3,2,1,0:T(8,128)(2,1)S(1)}, u32[]{:S(2)}, u32[]{:S(2)}) collective-permute-start(bf16[3,3,1,128,128]{4,3,2,1,0:T(8,128)(2,1)S(1)} %pad_maximum_fusion.6), channel_id=1, source_target_pairs={{1,0},{2,1},{3,2},{4,3},{5,4},{6,5},{7,6},{0,7},{9,8},{10,9},{11,1... | collective-permute-start | bytes 884744 | tf_op jit(solution)/shard_map/ppermute | solution.py:22
  159.9 12.6 %collective-permute-start.10 = (bf16[3,3,1,128,128]{4,3,2,1,0:T(8,128)(2,1)S(1)}, bf16[3,3,1,128,128]{4,3,2,1,0:T(8,128)(2,1)S(1)}, u32[]{:S(2)}, u32[]{:S(2)}) collective-permute-start(bf16[3,3,1,128,128]{4,3,2,1,0:T(8,128)(2,1)S(1)} %pad_maximum_fusion.6), channel_id=1, source_target_pairs={{0,1},{1,2},{2,3},{3,4},{4,5},{5,6},{6,7},{7,0},{8,9},{9,10},{10,1... | collective-permute-start | bytes 884744 | tf_op jit(solution)/shard_map/ppermute | solution.py:21
  331.6 16.3 %collective-permute-start.13 = (bf16[1,1,1,128,128]{4,3,2,1,0:T(8,128)(2,1)S(1)}, bf16[1,1,1,128,128]{4,3,2,1,0:T(8,128)(2,1)S(1)}, u32[]{:S(2)}, u32[]{:S(2)}) collective-permute-start(bf16[1,1,1,128,128]{4,3,2,1,0:T(8,128)(2,1)S(1)} %bitcast.201), channel_id=1, source_target_pairs={{64,0},{128,64},{192,128},{256,192},{320,256},{384,320},{448,384},... | collective-permute-start | bytes 98312 | tf_op jit(solution)/shard_map/ppermute | solution.py:22
  333.5 14.4 %collective-permute-start.12 = (bf16[1,1,1,128,128]{4,3,2,1,0:T(8,128)(2,1)S(1)}, bf16[1,1,1,128,128]{4,3,2,1,0:T(8,128)(2,1)S(1)}, u32[]{:S(2)}, u32[]{:S(2)}) collective-permute-start(bf16[1,1,1,128,128]{4,3,2,1,0:T(8,128)(2,1)S(1)} %bitcast.202), channel_id=1, source_target_pairs={{0,64},{64,128},{128,192},{192,256},{256,320},{320,384},{384,448},... | collective-permute-start | bytes 98312 | tf_op jit(solution)/shard_map/ppermute | solution.py:21
  348.0 6.6 collective-permute-start.15
  349.9 5.4 collective-permute-start.14
  356.1 11.0 %collective-permute-start.17 = (bf16[3,3,1,128,128]{4,3,2,1,0:T(8,128)(2,1)}, bf16[3,3,1,128,128]{4,3,2,1,0:T(8,128)(2,1)S(1)}, u32[]{:S(2)}, u32[]{:S(2)}) collective-permute-start(bf16[3,3,1,128,128]{4,3,2,1,0:T(8,128)(2,1)} %pad_maximum_fusion.7), channel_id=1, source_target_pairs={{1,0},{2,1},{3,2},{4,3},{5,4},{6,5},{7,6},{0,7},{9,8},{10,9},{11,1... | collective-permute-start | bytes 884744 | tf_op jit(solution)/shard_map/ppermute | solution.py:22
  359.5 14.3 %collective-permute-start.16 = (bf16[3,3,1,128,128]{4,3,2,1,0:T(8,128)(2,1)}, bf16[3,3,1,128,128]{4,3,2,1,0:T(8,128)(2,1)}, u32[]{:S(2)}, u32[]{:S(2)}) collective-permute-start(bf16[3,3,1,128,128]{4,3,2,1,0:T(8,128)(2,1)} %pad_maximum_fusion.7), channel_id=1, source_target_pairs={{0,1},{1,2},{2,3},{3,4},{4,5},{5,6},{6,7},{7,0},{8,9},{9,10},{10,1... | collective-permute-start | bytes 884744 | tf_op jit(solution)/shard_map/ppermute | solution.py:21
  (29 other events, 704.6 us)
Sparse Core Ops, SparseCore 0:
  38.9 278.0 all-reduce.7
  363.3 279.6 all-reduce.5
where the time goes:
time: 675 us; the launch traced here: 664 us
  waiting for transfers between devices  342 us (51%)
  blocking collectives  98.9 us (15%)
  matrix products  87.7 us (13%)
  starting transfers between devices  58.1 us (9%)
  other arithmetic  34.2 us (5%)
  local copies, waits for them, and re-layouts  18.9 us (3%)
  between operations  16.1 us (2%)
  loops' own time  7.66 us (1%)
    psum x1, waiting for transfers between devices, shards(): back_c, back_s = lax.psum((pull_c, pull_s), ('gx', 'gy', 'gz'))  200 us
    psum x1, waiting for transfers between devices, shards(): lax.psum((local_c, local_s, jnp.sum(charges, axis=1), jnp.sum(living)), (...  123 us
    psum x1, blocking collectives, shards(): lax.psum((local_c, local_s, jnp.sum(charges, axis=1), jnp.sum(living)), (...  98.9 us
    ppermute x9, starting transfers between devices, extended(): before = lax.ppermute(last, axis, up)  33.5 us
    dot_general x27, matrix products, add_force(): jnp.einsum('bic,jc->ibj', local_proj, near_rows, preferred_element_type=j...  26 us
    ppermute x9, starting transfers between devices, extended(): after = lax.ppermute(initial, axis, down)  24.6 us
    ppermute x9, waiting for transfers between devices, extended(): before = lax.ppermute(last, axis, up)  13.5 us
  transfers between devices with their start and end apart: 20, of which 7 were waited for; matrix products, arithmetic and copies ran while one was open for 16% of the time, Pallas kernels for 0%

commit v1 on v0

--- a/solution.py
+++ b/solution.py
@@ -107,7 +107,7 @@
     stacked_rows = jnp.concatenate([charges, living[None, :]], axis=0)
     local_c, local_s = structure(stacked_rows, absolute, wave_vec, wave_block)
     totals = lax.psum(
-        (local_c, local_s, jnp.sum(charges, axis=1), jnp.sum(living)), ("gx", "gy", "gz")
+        lax.psum((local_c, local_s, jnp.sum(charges, axis=1), jnp.sum(living)), ("gy", "gz")), "gx"
     )
     charge_mean = totals[2] / totals[3]
     neutral = (charges - charge_mean[:, None]) * living[None, :]

time: 675 us -> 1080 us (1.60)
  waiting for transfers between devices: 342 us -> 675 us
  blocking collectives: 98.9 us -> 153 us
  starting transfers between devices: 58.1 us -> 73.8 us
    psum x1, waiting for transfers between devices: 123 us -> 344 us  [shards(): lax.psum((local_c, local_s, jnp.sum(charges, axis=1), jnp.sum(living)), (...]
    psum x0 -> x1, waiting for transfers between devices: none -> 111 us  [shards(): lax.psum(lax.psum((local_c, local_s, jnp.sum(charges, axis=1), jnp.sum(li...]
    psum x0 -> x1, blocking collectives: none -> 39.4 us  [shards(): lax.psum(lax.psum((local_c, local_s, jnp.sum(charges, axis=1), jnp.sum(li...]
    ppermute x9, starting transfers between devices: 33.5 us -> 49.1 us  [extended(): before = lax.ppermute(last, axis, up)]
    psum x1, blocking collectives: 98.9 us -> 114 us  [shards(): lax.psum((local_c, local_s, jnp.sum(charges, axis=1), jnp.sum(living)), (...]
  transfers between devices with their start and end apart: 20 -> 21, of which waited for: 7 -> 7; matrix products, arithmetic and copies ran while one was open for 16% -> 10% of each run, Pallas kernels for 0% -> 0%
where the time goes in v1:
time: 1080 us; the launch traced here: 1070 us
  waiting for transfers between devices  675 us (62%)
  blocking collectives  153 us (14%)
  matrix products  87.7 us (8%)
  starting transfers between devices  73.8 us (7%)
  other arithmetic  34.2 us (3%)
  local copies, waits for them, and re-layouts  18.9 us (2%)
  between operations  15.8 us (1%)
    psum x1, waiting for transfers between devices, shards(): lax.psum((local_c, local_s, jnp.sum(charges, axis=1), jnp.sum(living)), (...  344 us
    psum x1, waiting for transfers between devices, shards(): back_c, back_s = lax.psum((pull_c, pull_s), ('gx', 'gy', 'gz'))  205 us
    psum x1, blocking collectives, shards(): lax.psum((local_c, local_s, jnp.sum(charges, axis=1), jnp.sum(living)), (...  114 us
    psum x1, waiting for transfers between devices, shards(): lax.psum(lax.psum((local_c, local_s, jnp.sum(charges, axis=1), jnp.sum(li...  111 us
    ppermute x9, starting transfers between devices, extended(): before = lax.ppermute(last, axis, up)  49.1 us
    psum x1, blocking collectives, shards(): lax.psum(lax.psum((local_c, local_s, jnp.sum(charges, axis=1), jnp.sum(li...  39.4 us
    dot_general x27, matrix products, add_force(): jnp.einsum('bic,jc->ibj', local_proj, near_rows, preferred_element_type=j...  26 us
    ppermute x9, starting transfers between devices, extended(): after = lax.ppermute(initial, axis, down)  24.1 us
  transfers between devices with their start and end apart: 21, of which 7 were waited for; matrix products, arithmetic and copies ran while one was open for 10% of the time, Pallas kernels for 0%

profile of v1, /device:TPU:23, one launch (start us, length us, event | category | flops | bytes accessed | tf_op | source)
XLA Modules:
  0.0 1066.0 jit_solution(7272354392614518872)
XLA Ops:
  7.2 6.4 collective-permute-start
  13.6 1.9 collective-permute-start.1
  17.1 6.6 collective-permute-start.7
  23.7 1.9 collective-permute-start.6
  39.9 113.6 %all-reduce.1 = (f32[64]{0:T(128)S(1)}, f32[]{:T(128)}) all-reduce(f32[64]{0:T(128)S(1)} %get-tuple-element.756, f32[]{:T(128)} %fusion.291), channel_id=1, replica_groups=mesh['gx'=8,'gy'=8,'gz'=8] {'gy','gz'}, use_global_device_ids=true, to_apply=%region_6.7 | all-reduce | flops 65 | bytes 520 | tf_op jit(solution)/shard_map/psum | solution.py:110
  153.5 39.4 %all-reduce.3 = (f32[64]{0:T(128)S(1)}, f32[]{:T(128)}) all-reduce(f32[64]{0:T(128)S(1)} %get-tuple-element.720, f32[]{:T(128)} %get-tuple-element.721), channel_id=1, replica_groups=mesh['gx'=8,'gy'=8,'gz'=8] {'gx'}, use_global_device_ids=true, to_apply=%region_7.8 | all-reduce | flops 65 | bytes 520 | tf_op jit(solution)/shard_map/psum | solution.py:109
  193.6 1.9 collective-permute-start.3
  195.5 16.4 %collective-permute-start.2 = (f32[3,1,1,3,128]{4,2,3,1,0:T(1,128)S(1)}, f32[3,1,1,3,128]{4,2,3,1,0:T(1,128)S(1)}, u32[]{:S(2)}, u32[]{:S(2)}) collective-permute-start(f32[3,1,1,3,128]{4,2,3,1,0:T(1,128)S(1)} %constant_dynamic-update-slice_fusion), channel_id=1, source_target_pairs={{0,8},{8,16},{16,24},{24,32},{32,40},{40,48},{48,56},{56,0},{1,9},... | collective-permute-start | bytes 13832 | tf_op jit(solution)/shard_map/ppermute | solution.py:21
  211.9 1.9 collective-permute-start.9
  213.9 4.6 collective-permute-start.8
  218.5 1.9 collective-permute-start.5
  220.4 4.7 collective-permute-start.4
  225.2 1.9 collective-permute-start.11
  227.1 5.8 collective-permute-start.10
  233.0 4.3 collective-permute-done.11
  237.3 3.5 collective-permute-done.10
  240.9 344.1 %all-reduce.11.cloned.1.call-done = (f32[65,2048]{1,0:T(8,128)}, f32[65,2048]{1,0:T(8,128)}) async-done(((f32[65,2048]{1,0:T(8,128)}, f32[65,2048]{1,0:T(8,128)}), (f32[65,2048]{1,0:T(8,128)}, f32[65,2048]{1,0:T(8,128)})) %all-reduce.11.cloned.1.call-update) | async-done | bytes 1064976 | tf_op jit(solution)/shard_map/psum | solution.py:110
  586.2 20.3 %while.36 = (s32[]{:T(128)}, f32[128,128]{1,0:T(8,128)S(1)}, f32[27,3,128]{2,1,0:T(4,128)S(1)}, f32[1,1,1,3,128]{4,3,2,1,0:T(4,128)S(1)}, bf16[27,128,128]{2,1,0...) while((s32[]{:T(128)}, f32[128,128]{1,0:T(8,128)S(1)}, ...), condition=%wide.region_2.3_spmd.clone.clone, body=%wide.region_0.0_spmd.clone.clone.sunk | while | flops 34161064 | bytes 826287 | solution.py:142
  606.7 111.3 %all-reduce.13.cloned.1.call-done = (f32[65,2048]{1,0:T(8,128)}, f32[65,2048]{1,0:T(8,128)}) async-done(((f32[65,2048]{1,0:T(8,128)}, f32[65,2048]{1,0:T(8,128)}), (f32[65,2048]{1,0:T(8,128)}, f32[65,2048]{1,0:T(8,128)})) %all-reduce.13.cloned.1.call-update) | async-done | bytes 1064976 | tf_op jit(solution)/shard_map/psum | solution.py:109
  719.7 1.4 fusion.48
  723.7 1.3 convolution_add_fusion.7
  726.3 1.3 convolution_add_fusion.5
  732.6 3.2 collective-permute-start.13
  735.8 3.4 collective-permute-start.12
  749.0 2.2 collective-permute-start.15
  751.1 3.1 collective-permute-start.14
  757.3 2.6 collective-permute-start.17
  759.9 2.9 collective-permute-start.16
  765.6 6.0 collective-permute-done.16
  771.6 2.0 pad_maximum_fusion.1
  773.6 67.3 %while.37 = (s32[]{:T(128)}, f32[3,128]{1,0:T(4,128)S(1)}, f32[27,3,128]{2,1,0:T(4,128)S(1)}, f32[1,1,1,3,128]{4,3,2,1,0:T(4,128)S(1)}, bf16[27,128,128]{2,1,0:T...) while((s32[]{:T(128)}, f32[3,128]{1,0:T(4,128)S(1)}, ...), condition=%wide.region_18.19_spmd.clone.clone, body=%wide.region_14.18_spmd.clone.clone.sunk | while | flops 51315852 | bytes 2604507 | solution.py:198
  840.9 204.6 %all-reduce.9.cloned.1.call-done = (f32[64,2048]{1,0:T(8,128)}, f32[64,2048]{1,0:T(8,128)}) async-done(((f32[64,2048]{1,0:T(8,128)}, f32[64,2048]{1,0:T(8,128)}), (f32[64,2048]{1,0:T(8,128)}, f32[64,2048]{1,0:T(8,128)})) %all-reduce.9.cloned.1.call-update) | async-done | bytes 1048592 | tf_op jit(solution)/shard_map/psum | solution.py:181
  (719 shorter events, 136.5 us)
Async XLA Ops:
  7.2 577.8 %all-reduce.11.cloned.1.call-start = ((), (), s32[]{:S(2)}) async-start(), calls=%async_computation.1 | async-start | bytes 2359296 | tf_op jit(solution)/shard_map/psum | solution.py:110
  7.2 186.3 %collective-permute-start = (f32[1,1,1,3,128]{4,2,3,1,0:T(1,128)}, f32[1,1,1,3,128]{4,2,3,1,0:T(1,128)S(1)}, u32[]{:S(2)}, u32[]{:S(2)}) collective-permute-start(f32[1,1,1,3,128]{4,2,3,1,0:T(1,128)} %param.19), channel_id=1, source_target_pairs={{0,64},{64,128},{128,192},{192,256},{256,320},{320,384},{384,448},... | collective-permute-start | bytes 4616 | tf_op jit(solution)/shard_map/ppermute | solution.py:21
  13.6 180.0 %collective-permute-start.1 = (f32[1,1,1,3,128]{4,2,3,1,0:T(1,128)}, f32[1,1,1,3,128]{4,2,3,1,0:T(1,128)S(1)}, u32[]{:S(2)}, u32[]{:S(2)}) collective-permute-start(f32[1,1,1,3,128]{4,2,3,1,0:T(1,128)} %param.19), channel_id=1, source_target_pairs={{64,0},{128,64},{192,128},{256,192},{320,256},{384,320},{448,384},... | collective-permute-start | bytes 4616 | tf_op jit(solution)/shard_map/ppermute | solution.py:22
  17.1 194.8 %collective-permute-start.7 = (bf16[1,1,1,128,128]{4,3,2,1,0:T(8,128)(2,1)S(1)}, bf16[1,1,1,128,128]{4,3,2,1,0:T(8,128)(2,1)S(1)}, u32[]{:S(2)}, u32[]{:S(2)}) collective-permute-start(bf16[1,1,1,128,128]{4,3,2,1,0:T(8,128)(2,1)S(1)} %broadcast_multiply_fusion.2), channel_id=1, source_target_pairs={{64,0},{128,64},{192,128},{256,192},{320,256},{384,320},{448,384},... | collective-permute-start | bytes 98312 | tf_op jit(solution)/shard_map/ppermute | solution.py:22
  23.7 188.2 %collective-permute-start.6 = (bf16[1,1,1,128,128]{4,3,2,1,0:T(8,128)(2,1)S(1)}, bf16[1,1,1,128,128]{4,3,2,1,0:T(8,128)(2,1)S(1)}, u32[]{:S(2)}, u32[]{:S(2)}) collective-permute-start(bf16[1,1,1,128,128]{4,3,2,1,0:T(8,128)(2,1)S(1)} %broadcast_multiply_fusion.2), channel_id=1, source_target_pairs={{0,64},{64,128},{128,192},{192,256},{256,320},{320,384},{384,448},... | collective-permute-start | bytes 98312 | tf_op jit(solution)/shard_map/ppermute | solution.py:21
  25.9 717.2 %copy-start.26 = (f32[1,512]{1,0:T(1,128)}, f32[1,512]{1,0:T(1,128)S(1)}, u32[]{:S(2)}) copy-start(f32[1,512]{1,0:T(1,128)S(1)} %get-tuple-element.741) | copy-start | bytes 6148
  25.9 718.4 %copy-start.8 = (f32[1,512]{1,0:T(1,128)}, f32[1,512]{1,0:T(1,128)S(1)}, u32[]{:S(2)}) copy-start(f32[1,512]{1,0:T(1,128)S(1)} %get-tuple-element.742) | copy-start | bytes 6148
  25.9 718.4 %copy-start.10 = (f32[1,512]{1,0:T(1,128)}, f32[1,512]{1,0:T(1,128)S(1)}, u32[]{:S(2)}) copy-start(f32[1,512]{1,0:T(1,128)S(1)} %get-tuple-element.743) | copy-start | bytes 6148
  25.9 718.4 %copy-start.12 = (f32[1,512]{1,0:T(1,128)}, f32[1,512]{1,0:T(1,128)S(1)}, u32[]{:S(2)}) copy-start(f32[1,512]{1,0:T(1,128)S(1)} %get-tuple-element.744) | copy-start | bytes 6148
  25.9 719.7 %copy-start.14 = (f32[1,512]{1,0:T(1,128)}, f32[1,512]{1,0:T(1,128)S(1)}, u32[]{:S(2)}) copy-start(f32[1,512]{1,0:T(1,128)S(1)} %get-tuple-element.745) | copy-start | bytes 6148
  25.9 719.7 %copy-start.16 = (f32[1,512]{1,0:T(1,128)}, f32[1,512]{1,0:T(1,128)S(1)}, u32[]{:S(2)}) copy-start(f32[1,512]{1,0:T(1,128)S(1)} %get-tuple-element.746) | copy-start | bytes 6148
  25.9 719.7 %copy-start.18 = (f32[1,512]{1,0:T(1,128)}, f32[1,512]{1,0:T(1,128)S(1)}, u32[]{:S(2)}) copy-start(f32[1,512]{1,0:T(1,128)S(1)} %get-tuple-element.747) | copy-start | bytes 6148
  25.9 721.7 %copy-start.20 = (f32[1,512]{1,0:T(1,128)}, f32[1,512]{1,0:T(1,128)S(1)}, u32[]{:S(2)}) copy-start(f32[1,512]{1,0:T(1,128)S(1)} %get-tuple-element.748) | copy-start | bytes 6148
  26.0 721.7 %copy-start.22 = (f32[1,512]{1,0:T(1,128)}, f32[1,512]{1,0:T(1,128)S(1)}, u32[]{:S(2)}) copy-start(f32[1,512]{1,0:T(1,128)S(1)} %get-tuple-element.749) | copy-start | bytes 6148
  26.0 721.7 %copy-start.24 = (f32[1,512]{1,0:T(1,128)}, f32[1,512]{1,0:T(1,128)S(1)}, u32[]{:S(2)}) copy-start(f32[1,512]{1,0:T(1,128)S(1)} %get-tuple-element.750) | copy-start | bytes 6148
  26.8 727.5 %copy-start.5 = (f32[128]{0:T(128)}, f32[128]{0:T(128)S(1)}, u32[]{:S(2)}) copy-start(f32[128]{0:T(128)S(1)} %get-tuple-element.755) | copy-start | bytes 1540
  38.8 679.2 %all-reduce.13.cloned.1.call-start = ((), (), s32[]{:S(2)}) async-start(), calls=%async_computation.2 | async-start | bytes 2359296 | tf_op jit(solution)/shard_map/psum | solution.py:109
  193.6 24.8 %collective-permute-start.3 = (f32[3,1,1,3,128]{4,2,3,1,0:T(1,128)S(1)}, f32[3,1,1,3,128]{4,2,3,1,0:T(1,128)S(1)}, u32[]{:S(2)}, u32[]{:S(2)}) collective-permute-start(f32[3,1,1,3,128]{4,2,3,1,0:T(1,128)S(1)} %constant_dynamic-update-slice_fusion), channel_id=1, source_target_pairs={{8,0},{16,8},{24,16},{32,24},{40,32},{48,40},{56,48},{0,56},{9,1},... | collective-permute-start | bytes 13832 | tf_op jit(solution)/shard_map/ppermute | solution.py:22
  195.5 22.9 %collective-permute-start.2 = (f32[3,1,1,3,128]{4,2,3,1,0:T(1,128)S(1)}, f32[3,1,1,3,128]{4,2,3,1,0:T(1,128)S(1)}, u32[]{:S(2)}, u32[]{:S(2)}) collective-permute-start(f32[3,1,1,3,128]{4,2,3,1,0:T(1,128)S(1)} %constant_dynamic-update-slice_fusion), channel_id=1, source_target_pairs={{0,8},{8,16},{16,24},{24,32},{32,40},{40,48},{48,56},{56,0},{1,9},... | collective-permute-start | bytes 13832 | tf_op jit(solution)/shard_map/ppermute | solution.py:21
  211.9 13.1 %collective-permute-start.9 = (bf16[3,1,1,128,128]{4,3,2,1,0:T(8,128)(2,1)S(1)}, bf16[3,1,1,128,128]{4,3,2,1,0:T(8,128)(2,1)S(1)}, u32[]{:S(2)}, u32[]{:S(2)}) collective-permute-start(bf16[3,1,1,128,128]{4,3,2,1,0:T(8,128)(2,1)S(1)} %pad_maximum_fusion.12), channel_id=1, source_target_pairs={{8,0},{16,8},{24,16},{32,24},{40,32},{48,40},{56,48},{0,56},{9,1},... | collective-permute-start | bytes 294920 | tf_op jit(solution)/shard_map/ppermute | solution.py:22
  213.9 11.2 %collective-permute-start.8 = (bf16[3,1,1,128,128]{4,3,2,1,0:T(8,128)(2,1)S(1)}, bf16[3,1,1,128,128]{4,3,2,1,0:T(8,128)(2,1)S(1)}, u32[]{:S(2)}, u32[]{:S(2)}) collective-permute-start(bf16[3,1,1,128,128]{4,3,2,1,0:T(8,128)(2,1)S(1)} %pad_maximum_fusion.12), channel_id=1, source_target_pairs={{0,8},{8,16},{16,24},{24,32},{32,40},{40,48},{48,56},{56,0},{1,9},... | collective-permute-start | bytes 294920 | tf_op jit(solution)/shard_map/ppermute | solution.py:21
  218.5 14.4 %collective-permute-start.5 = (f32[3,3,1,3,128]{4,2,3,1,0:T(1,128)S(1)}, f32[3,3,1,3,128]{4,2,3,1,0:T(1,128)S(1)}, u32[]{:S(2)}, u32[]{:S(2)}) collective-permute-start(f32[3,3,1,3,128]{4,2,3,1,0:T(1,128)S(1)} %pad_maximum_fusion.17), channel_id=1, source_target_pairs={{1,0},{2,1},{3,2},{4,3},{5,4},{6,5},{7,6},{0,7},{9,8},{10,9},{11,1... | collective-permute-start | bytes 41480 | tf_op jit(solution)/shard_map/ppermute | solution.py:22
  220.4 12.5 %collective-permute-start.4 = (f32[3,3,1,3,128]{4,2,3,1,0:T(1,128)S(1)}, f32[3,3,1,3,128]{4,2,3,1,0:T(1,128)S(1)}, u32[]{:S(2)}, u32[]{:S(2)}) collective-permute-start(f32[3,3,1,3,128]{4,2,3,1,0:T(1,128)S(1)} %pad_maximum_fusion.17), channel_id=1, source_target_pairs={{0,1},{1,2},{2,3},{3,4},{4,5},{5,6},{6,7},{7,0},{8,9},{9,10},{10,1... | collective-permute-start | bytes 41480 | tf_op jit(solution)/shard_map/ppermute | solution.py:21
  225.2 12.1 %collective-permute-start.11 = (bf16[3,3,1,128,128]{4,3,2,1,0:T(8,128)(2,1)S(1)}, bf16[3,3,1,128,128]{4,3,2,1,0:T(8,128)(2,1)S(1)}, u32[]{:S(2)}, u32[]{:S(2)}) collective-permute-start(bf16[3,3,1,128,128]{4,3,2,1,0:T(8,128)(2,1)S(1)} %pad_maximum_fusion.6), channel_id=1, source_target_pairs={{1,0},{2,1},{3,2},{4,3},{5,4},{6,5},{7,6},{0,7},{9,8},{10,9},{11,1... | collective-permute-start | bytes 884744 | tf_op jit(solution)/shard_map/ppermute | solution.py:22
  227.1 13.7 %collective-permute-start.10 = (bf16[3,3,1,128,128]{4,3,2,1,0:T(8,128)(2,1)S(1)}, bf16[3,3,1,128,128]{4,3,2,1,0:T(8,128)(2,1)S(1)}, u32[]{:S(2)}, u32[]{:S(2)}) collective-permute-start(bf16[3,3,1,128,128]{4,3,2,1,0:T(8,128)(2,1)S(1)} %pad_maximum_fusion.6), channel_id=1, source_target_pairs={{0,1},{1,2},{2,3},{3,4},{4,5},{5,6},{6,7},{7,0},{8,9},{9,10},{10,1... | collective-permute-start | bytes 884744 | tf_op jit(solution)/shard_map/ppermute | solution.py:21
  585.0 460.5 %all-reduce.9.cloned.1.call-start = ((), (), s32[]{:S(2)}) async-start(), calls=%async_computation | async-start | bytes 2097152 | tf_op jit(solution)/shard_map/psum | solution.py:181
  732.6 16.3 %collective-permute-start.13 = (bf16[1,1,1,128,128]{4,3,2,1,0:T(8,128)(2,1)S(1)}, bf16[1,1,1,128,128]{4,3,2,1,0:T(8,128)(2,1)S(1)}, u32[]{:S(2)}, u32[]{:S(2)}) collective-permute-start(bf16[1,1,1,128,128]{4,3,2,1,0:T(8,128)(2,1)S(1)} %bitcast.201), channel_id=1, source_target_pairs={{64,0},{128,64},{192,128},{256,192},{320,256},{384,320},{448,384},... | collective-permute-start | bytes 98312 | tf_op jit(solution)/shard_map/ppermute | solution.py:22
  735.8 13.1 %collective-permute-start.12 = (bf16[1,1,1,128,128]{4,3,2,1,0:T(8,128)(2,1)S(1)}, bf16[1,1,1,128,128]{4,3,2,1,0:T(8,128)(2,1)S(1)}, u32[]{:S(2)}, u32[]{:S(2)}) collective-permute-start(bf16[1,1,1,128,128]{4,3,2,1,0:T(8,128)(2,1)S(1)} %bitcast.202), channel_id=1, source_target_pairs={{0,64},{64,128},{128,192},{192,256},{256,320},{320,384},{384,448},... | collective-permute-start | bytes 98312 | tf_op jit(solution)/shard_map/ppermute | solution.py:21
  749.0 6.6 collective-permute-start.15
  751.1 5.5 collective-permute-start.14
  757.3 8.3 collective-permute-start.17
  759.9 11.7 %collective-permute-start.16 = (bf16[3,3,1,128,128]{4,3,2,1,0:T(8,128)(2,1)}, bf16[3,3,1,128,128]{4,3,2,1,0:T(8,128)(2,1)}, u32[]{:S(2)}, u32[]{:S(2)}) collective-permute-start(bf16[3,3,1,128,128]{4,3,2,1,0:T(8,128)(2,1)} %pad_maximum_fusion.7), channel_id=1, source_target_pairs={{0,1},{1,2},{2,3},{3,4},{4,5},{5,6},{6,7},{7,0},{8,9},{9,10},{10,1... | collective-permute-start | bytes 884744 | tf_op jit(solution)/shard_map/ppermute | solution.py:21
  (30 other events, 2223.7 us)
Sparse Core Ops, SparseCore 0:
  38.9 545.9 all-reduce.10
  588.0 129.9 all-reduce.12
  764.5 280.8 all-reduce.8
